TPU v7x, 128 devices: a whole 4x4x4 slice. The times are simulated.
128 devices in a mesh: slab: 4 (over y_hi, core), orb: 8 (over x, y_lo), pois: 4 (over z).
Axes of the slice: x: 4, y: 4 (y_hi: 2, y_lo: 2; y = y_hi * 2 + y_lo), z: 4, core: 2. Of those that a mesh axis runs over, the one named last changes fastest.
Arguments:
- orbitals: bfloat16 [32, 2, 192, 128, 128], P('orb', None, 'slab', 'pois'), may hold values from -8 to 8
- occupations: float32 [32], P('orb'), may hold values from 5e-05 to 0.0005
- ext_pot: float32 [192, 128, 128], P('slab', 'pois'), may hold values from -1 to 1
- hartree_old: float32 [192, 128, 128], P('slab', 'pois'), may hold values from 0 to 2
Outputs:
- orbitals_new: float32 [32, 2, 192, 128, 128], P('orb', None, 'slab', 'pois')
- hartree_new: float32 [192, 128, 128], P('slab', 'pois', 'orb')
All inputs are finite; a program needn't handle non-finite values.
Results may differ from a plain program's by a relative error of at most 0.0003.
Values may be sent and summed in bfloat16 or wider, within the bound.
No kernel may reach another device: no remote copies, remote signals or barrier semaphores. Data moves between devices by JAX's collectives and lax.ppermute only.
A program may use at most 64 MiB of HBM per device.

v0:
```python
import jax
import jax.numpy as jnp
from jax import lax
from jax.sharding import PartitionSpec as P

NX = 192
NY = 128
NZ = 128


time_step = 0.3


def extended(cells, sides, width):
    for axis, dim in sides:
        count = lax.axis_size(axis)
        ends = count - 1
        head = lax.slice_in_dim(cells, 0, width, axis=dim)
        tail = lax.slice_in_dim(cells, cells.shape[dim] - width, cells.shape[dim], axis=dim)
        cells = jnp.concatenate(
            [
                lax.ppermute(tail, axis, [(i, (i + 1) % count) for i in range(ends)]),
                cells,
                lax.ppermute(head, axis, [((i + 1) % count, i) for i in range(ends)]),
            ],
            axis=dim,
        )
    return cells


def sine_table(row_count, col_start, col_count, length):
    row_index = lax.iota(jnp.int32, row_count) + 1
    col_index = col_start + lax.iota(jnp.int32, col_count) + 1
    product = row_index[:, None] * col_index[None, :] % (2 * (length + 1))
    return jnp.sin(jnp.pi * product.astype(jnp.float32) / (length + 1))


def eigen_values(first_mode, mode_count, length):
    mode_index = first_mode + lax.iota(jnp.int32, mode_count) + 1
    return 2.0 - 2.0 * jnp.cos(jnp.pi * mode_index.astype(jnp.float32) / (length + 1))


def hamiltonian(padded, potential):
    center = padded[:, :, 1:-1, 1:-1, :].astype(jnp.float32)
    z_padded = jnp.pad(center, ((0, 0), (0, 0), (0, 0), (0, 0), (1, 1)))
    beside_all = padded[:, :, 2:, 1:-1, :].astype(jnp.float32) + padded[:, :, :-2, 1:-1, :].astype(
        jnp.float32
    )
    beside_all = (
        beside_all
        + padded[:, :, 1:-1, 2:, :].astype(jnp.float32)
        + padded[:, :, 1:-1, :-2, :].astype(jnp.float32)
    )
    beside_all = beside_all + z_padded[..., 2:] + z_padded[..., :-2]
    return (3.0 + potential) * center - 0.5 * beside_all


def plane_sine(spectrum):
    highest = lax.Precision.HIGHEST
    width_c, width_x, width_y = spectrum.shape
    slab_start = lax.axis_index("slab") * width_x
    pois_start = lax.axis_index("pois") * width_y
    sines_x = sine_table(NX, slab_start, width_x, NX)
    sines_y = sine_table(NY, pois_start, width_y, NY)
    partial_sum = jnp.einsum("ax,cxy->ayc", sines_x, spectrum, precision=highest)
    full_sum = jnp.einsum("by,ayc->abc", sines_y, partial_sum, precision=highest)
    row_blocks = full_sum.reshape(NX // width_x, width_x, NY // width_y, width_y, width_c)
    row_blocks = jnp.transpose(row_blocks, (0, 2, 1, 3, 4)).reshape(-1, width_c)
    result_rows = lax.psum_scatter(row_blocks, ("slab", "pois"), scatter_dimension=0, tiled=True)
    return result_rows.reshape(width_x, width_y, width_c)


def body(orbitals, occupations, ext_pot, hartree_old):
    highest = lax.Precision.HIGHEST
    width_x = orbitals.shape[2]
    width_y = orbitals.shape[3]
    padded = extended(orbitals, (("slab", 2), ("pois", 3)), 1)
    center = padded[:, :, 1:-1, 1:-1, :].astype(jnp.float32)

    def first_image(potential):
        image_one = hamiltonian(padded, potential)
        image_padded = extended(image_one, (("slab", 2), ("pois", 3)), 1)
        return (image_one, image_padded)

    def taylor_step(potential):
        image_one, image_padded = first_image(potential)
        image_two = hamiltonian(image_padded, potential)
        rotated = jnp.stack([image_one[:, 1], -image_one[:, 0]], axis=1)
        return center + time_step * rotated - 0.5 * time_step * time_step * image_two

    pot_start = ext_pot + hartree_old
    predicted = taylor_step(pot_start)
    density_part = jnp.sum(
        occupations[:, None, None, None]
        * (predicted[:, 0] * predicted[:, 0] + predicted[:, 1] * predicted[:, 1]),
        axis=0,
    )
    total = lax.psum(jnp.sum(density_part), ("slab", "orb", "pois"))
    density_part = density_part - total / (NX * NY * NZ) / lax.axis_size("orb")
    full_z = density_part.shape[2]
    width_z = full_z // lax.axis_size("orb")
    sines = sine_table(lax.axis_size("orb") * width_z, 0, full_z, full_z)
    spectrum = lax.psum_scatter(
        jnp.einsum("cz,xyz->cxy", sines, density_part, precision=highest),
        "orb",
        scatter_dimension=0,
        tiled=True,
    )
    spectrum = plane_sine(spectrum)
    slab_start = lax.axis_index("slab") * width_x
    pois_start = lax.axis_index("pois") * width_y
    orb_start = lax.axis_index("orb") * width_z
    divisor = (
        eigen_values(slab_start, width_x, NX)[:, None, None]
        + eigen_values(pois_start, width_y, NY)[None, :, None]
        + eigen_values(orb_start, width_z, NZ)[None, None, :]
    )
    factor = 32.0 * jnp.pi / ((NX + 1) * (NY + 1) * (NZ + 1))
    scaled = jnp.transpose(spectrum * factor / divisor, (2, 0, 1))
    field_part = plane_sine(scaled)
    section = lax.all_gather(field_part, "orb", axis=2, tiled=True)
    sines = sine_table(full_z, jnp.int32(0), section.shape[2], full_z)
    hartree_full = jnp.einsum("zc,xyc->xyz", sines, section, precision=highest)
    pot_middle = ext_pot + 0.5 * (hartree_old + hartree_full)
    orbitals_new = taylor_step(pot_middle)
    hartree_new = lax.dynamic_slice_in_dim(hartree_full, orb_start, width_z, 2)
    return (orbitals_new, hartree_new)


def solution(mesh):
    placed = (
        P("orb", None, "slab", "pois", None),
        P("orb"),
        P("slab", "pois", None),
        P("slab", "pois", None),
    )
    return jax.shard_map(
        body,
        mesh=mesh,
        in_specs=placed,
        out_specs=(P("orb", None, "slab", "pois", None), P("slab", "pois", "orb")),
        check_vma=False,
    )
```

profile of v0, /device:TPU:1, one launch (start us, length us, event | category | flops | bytes accessed | tf_op | source)
XLA Modules:
  0.0 536.6 jit_solution(13242921233021301441)
XLA Ops:
  7.2 3.3 fusion.118
  10.8 3.4 collective-permute-start
  14.2 4.8 collective-permute-start.1
  21.1 3.5 collective-permute-start.3
  24.6 1.3 collective-permute-start.2
  26.6 3.8 collective-permute-done.2
  30.4 10.8 %multiply_subtract_fusion.1 = (f32[4,2,48,32,128]{4,2,3,1,0:T(8,128)S(1)}, f32[4,2,48,32,128]{4,2,3,1,0:T(8,128)}) fusion(f32[48,32,128]{2,0,1:T(8,128)S(1)} %copy.45, bf16[4,2,48,32,128]{4,3,2,1,0:T(8,128)(2,1)S(1)} %copy-done.2, f32[4,2,48,32,128]{4,2,3,1,0:T(8,128)S(1)} %get-tuple-element.33, bf16[4,2,1,32,128]{4,2,3,1,0:T(2,128)(2,1)S(1)} %collective-permute-done, ...), kind=kLoop, calls=%fused_computation.48 | loop fusion | flops 51904512 | bytes 26288128 | tf_op jit(solution)/shard_map/sub | solution.py:55
  41.4 1.9 collective-permute-start.4
  43.3 7.1 %collective-permute-start.5 = (f32[4,2,1,32,128]{4,3,2,1,0:T(8,128)S(1)}, f32[4,2,1,32,128]{4,3,2,1,0:T(8,128)S(1)}, u32[]{:S(2)}, u32[]{:S(2)}) collective-permute-start(f32[4,2,1,32,128]{4,3,2,1,0:T(8,128)S(1)} %bitcast.77), channel_id=1, source_target_pairs={{0,32},{32,64},{64,96},{1,33},{33,65},{65,97},{2,34},{34,66},{66,9... | collective-permute-start | bytes 393224 | tf_op jit(solution)/shard_map/ppermute | solution.py:22
  52.4 3.6 collective-permute-start.7
  56.0 1.3 collective-permute-start.6
  58.9 3.8 collective-permute-done.6
  62.8 9.9 %fusion.8 = f32[4,2,48,32,128]{4,2,3,1,0:T(8,128)S(1)} fusion(f32[4,2,48,32,128]{4,2,3,1,0:T(8,128)S(1)} %get-tuple-element.14, f32[4,2,50,1,128]{4,2,3,1,0:T(8,128)S(1)} %collective-permute-done.7, f32[4,2,1,32,128]{4,2,3,1,0:T(1,128)S(1)} %bitcast.73, f32[4,2,1,32,128]{4,2,3,1,0:T(1,128)S(1)} %bitcast.75, ...), kind=kLoop, calls=%fused_computation.14 | loop fusion | flops 34603008 | bytes 23478272 | tf_op jit(solution)/shard_map/sub | solution.py:89
  72.7 2.1 fusion.110
  74.8 67.3 %psum.7 = f32[]{:T(128)} all-reduce(f32[]{:T(128)} %get-tuple-element.12), channel_id=1, replica_groups=mesh['slab'=4,'orb'=8,'pois'=4] {'slab','orb','pois'}, use_global_device_ids=true, to_apply=%region_2.3 | all-reduce | flops 1 | bytes 8 | tf_op jit(solution)/shard_map/psum | solution.py:98
  142.8 1.4 copy_subtract_fusion
  144.2 4.7 fusion.26
  149.0 47.2 %reduce-scatter.4.cloned.1.call-done = f32[16,48,32]{1,0,2:T(8,128)} async-done(((f32[128,48,32]{1,0,2:T(8,128)}), f32[16,48,32]{1,0,2:T(8,128)}) %reduce-scatter.4.cloned.1.call-update) | async-done | bytes 98320 | tf_op jit(solution)/shard_map/reduce_scatter | solution.py:103
  196.2 2.6 convolution_bitcast_fusion.3
  198.8 2.9 copy.60
  201.7 4.1 convolution_bitcast_fusion.1
  205.8 3.1 copy.61
  208.8 5.4 reshape.112
  214.2 7.1 %copy.62 = f32[4,4,48,32,16]{3,2,1,0,4:T(8,128)} copy(f32[4,4,48,32,16]{2,0,4,3,1:T(4,128)} %bitcast.66) | data formatting | bytes 3145728 | tf_op jit(solution)/shard_map/transpose | solution.py:68
  221.3 5.6 %reshape.113 = f32[24576,16]{0,1:T(8,128)} reshape(f32[4,4,48,32,16]{3,2,1,0,4:T(8,128)} %copy.62) | data formatting | bytes 3145728 | tf_op jit(solution)/shard_map/reshape | solution.py:68
  228.6 68.1 %reduce-scatter.6.cloned.1.call-done = f32[1536,16]{0,1:T(8,128)} async-done(((f32[24576,16]{0,1:T(8,128)}), f32[1536,16]{0,1:T(8,128)}) %reduce-scatter.6.cloned.1.call-update) | async-done | bytes 98320 | tf_op jit(solution)/shard_map/reduce_scatter | solution.py:69
  296.7 1.5 broadcast_multiply_fusion
  299.2 2.6 convolution_bitcast_fusion.2
  301.8 2.9 copy.64
  304.8 4.1 convolution_bitcast_fusion
  308.8 3.1 copy.65
  311.9 5.4 reshape.114
  317.2 7.1 %copy.66 = f32[4,4,48,32,16]{3,2,1,0,4:T(8,128)} copy(f32[4,4,48,32,16]{2,0,4,3,1:T(4,128)} %bitcast.67) | data formatting | bytes 3145728 | tf_op jit(solution)/shard_map/transpose | solution.py:68
  324.3 5.6 %reshape.115 = f32[24576,16]{0,1:T(8,128)} reshape(f32[4,4,48,32,16]{3,2,1,0,4:T(8,128)} %copy.66) | data formatting | bytes 3145728 | tf_op jit(solution)/shard_map/reshape | solution.py:68
  330.0 68.2 %reduce-scatter.8.cloned.1.call-done = f32[1536,16]{0,1:T(8,128)} async-done(((f32[24576,16]{0,1:T(8,128)}), f32[1536,16]{0,1:T(8,128)}) %reduce-scatter.8.cloned.1.call-update) | async-done | bytes 98320 | tf_op jit(solution)/shard_map/reduce_scatter | solution.py:69
  399.3 60.6 %all_gather.3 = f32[48,32,128]{1,2,0:T(8,128)S(1)} all-gather(f32[48,32,16]{1,2,0:T(8,128)S(1)} %copy.67), channel_id=1, replica_groups=mesh['slab'=4,'orb'=8,'pois'=4] {'orb'}, dimensions={2}, use_global_device_ids=true | all-gather | bytes 884736 | tf_op jit(solution)/shard_map/all_gather | solution.py:121
  459.9 7.4 %add_add_fusion = (f32[48,32,128]{2,1,0:T(8,128)S(1)}, f32[48,32,128]{2,1,0:T(8,128)}) fusion(f32[48,32,128]{2,1,0:T(8,128)} %param.6, f32[48,32,128]{2,1,0:T(8,128)} %param.7, f32[48,32,128]{1,2,0:T(8,128)S(1)} %all_gather.3, s32[128]{0:T(128)S(1)} %iota_add_fusion.1), kind=kOutput, calls=%fused_computation.71 | convolution fusion | flops 302923776 | bytes 3932672 | tf_op jit(solution)/shard_map/zc,xyc->xyz/dot_general | solution.py:123
  467.8 4.5 multiply_subtract_fusion
  472.4 2.7 copy-done
  476.0 6.7 %collective-permute-start.8 = (f32[4,2,1,32,128]{4,3,2,1,0:T(8,128)}, f32[4,2,1,32,128]{4,3,2,1,0:T(8,128)S(1)}, u32[]{:S(2)}, u32[]{:S(2)}) collective-permute-start(f32[4,2,1,32,128]{4,3,2,1,0:T(8,128)} %bitcast.17), channel_id=1, source_target_pairs={{32,0},{64,32},{96,64},{33,1},{65,33},{97,65},{34,2},{66,34},{98,6... | collective-permute-start | bytes 393224 | tf_op jit(solution)/shard_map/ppermute | solution.py:24
  482.7 3.7 collective-permute-start.9
  488.4 1.9 pad_maximum_fusion.26
  490.3 2.5 collective-permute-start.11
  492.8 1.4 collective-permute-start.10
  494.2 3.3 fusion.113
  498.7 2.2 copy.76
  500.9 24.1 %fusion.14 = f32[4,2,48,32,128]{4,2,3,1,0:T(8,128)S(1)} fusion(f32[4,2,48,32,128]{4,2,3,1,0:T(8,128)} %copy-done, f32[4,2,50,1,128]{4,2,3,1,0:T(8,128)} %collective-permute-done.11, f32[4,2,1,32,128]{4,2,3,1,0:T(1,128)S(1)} %bitcast.69, f32[4,2,1,32,128]{4,2,3,1,0:T(1,128)S(1)} %bitcast.71, f32[4,2,50,1,128]{4,2,3,1,0:T(8,128)} %collective-permute-done.10, ...), kind=kLoop, calls=%fused_computation.20 | loop fusion | flops 34603008 | bytes 23478272 | tf_op jit(solution)/shard_map/sub | solution.py:89
  525.1 4.6 copy.75
  (52 shorter events, 15.2 us)
Async XLA Ops:
  7.2 189.0 %reduce-scatter.4.cloned.1.call-start = ((), (), s32[]{:S(2)}) async-start(), calls=%async_computation.3 | async-start | bytes 2359296 | tf_op jit(solution)/shard_map/reduce_scatter | solution.py:103
  7.2 18.7 %copy-start.5 = (f32[48,32,128]{2,1,0:T(8,128)S(1)}, f32[48,32,128]{2,1,0:T(8,128)}, u32[]{:S(2)}) copy-start(f32[48,32,128]{2,1,0:T(8,128)} %param.6) | copy-start | bytes 2359300
  7.2 18.7 %copy-start.6 = (f32[48,32,128]{2,1,0:T(8,128)S(1)}, f32[48,32,128]{2,1,0:T(8,128)}, u32[]{:S(2)}) copy-start(f32[48,32,128]{2,1,0:T(8,128)} %param.7) | copy-start | bytes 2359300
  10.5 19.8 %copy-start.2 = (bf16[4,2,48,32,128]{4,3,2,1,0:T(8,128)(2,1)S(1)}, bf16[4,2,48,32,128]{4,3,2,1,0:T(8,128)(2,1)}, u32[]{:S(2)}) copy-start(bf16[4,2,48,32,128]{4,3,2,1,0:T(8,128)(2,1)} %param.4) | copy-start | bytes 9437188
  10.8 9.0 %collective-permute-start = (bf16[4,2,1,32,128]{4,2,3,1,0:T(2,128)(2,1)S(1)}, bf16[4,2,1,32,128]{4,2,3,1,0:T(2,128)(2,1)S(1)}, u32[]{:S(2)}, u32[]{:S(2)}) collective-permute-start(bf16[4,2,1,32,128]{4,2,3,1,0:T(2,128)(2,1)S(1)} %get-tuple-element.31), channel_id=1, source_target_pairs={{32,0},{64,32},{96,64},{33,1},{65,33},{97,65},{34,2},{66,34},{98,6... | collective-permute-start | bytes 196616 | tf_op jit(solution)/shard_map/ppermute | solution.py:24
  14.2 6.8 %collective-permute-start.1 = (bf16[4,2,1,32,128]{4,2,3,1,0:T(2,128)(2,1)S(1)}, bf16[4,2,1,32,128]{4,2,3,1,0:T(2,128)(2,1)S(1)}, u32[]{:S(2)}, u32[]{:S(2)}) collective-permute-start(bf16[4,2,1,32,128]{4,2,3,1,0:T(2,128)(2,1)S(1)} %get-tuple-element.30), channel_id=1, source_target_pairs={{0,32},{32,64},{64,96},{1,33},{33,65},{65,97},{2,34},{34,66},{66,9... | collective-permute-start | bytes 196616 | tf_op jit(solution)/shard_map/ppermute | solution.py:22
  21.1 5.5 %collective-permute-start.3 = (bf16[4,2,50,1,128]{4,2,3,1,0:T(8,128)(2,1)S(1)}, bf16[4,2,50,1,128]{4,2,3,1,0:T(8,128)(2,1)S(1)}, u32[]{:S(2)}, u32[]{:S(2)}) collective-permute-start(bf16[4,2,50,1,128]{4,2,3,1,0:T(8,128)(2,1)S(1)} %get-tuple-element.29), channel_id=1, source_target_pairs={{0,1},{1,2},{2,3},{4,5},{5,6},{6,7},{8,9},{9,10},{10,11},{12,13},{... | collective-permute-start | bytes 307208 | tf_op jit(solution)/shard_map/ppermute | solution.py:22
  24.6 5.7 %collective-permute-start.2 = (bf16[4,2,50,1,128]{4,2,3,1,0:T(8,128)(2,1)S(1)}, bf16[4,2,50,1,128]{4,2,3,1,0:T(8,128)(2,1)S(1)}, u32[]{:S(2)}, u32[]{:S(2)}) collective-permute-start(bf16[4,2,50,1,128]{4,2,3,1,0:T(8,128)(2,1)S(1)} %get-tuple-element.28), channel_id=1, source_target_pairs={{1,0},{2,1},{3,2},{5,4},{6,5},{7,6},{9,8},{10,9},{11,10},{13,12},{... | collective-permute-start | bytes 307208 | tf_op jit(solution)/shard_map/ppermute | solution.py:24
  41.4 9.8 %collective-permute-start.4 = (f32[4,2,1,32,128]{4,3,2,1,0:T(8,128)S(1)}, f32[4,2,1,32,128]{4,3,2,1,0:T(8,128)S(1)}, u32[]{:S(2)}, u32[]{:S(2)}) collective-permute-start(f32[4,2,1,32,128]{4,3,2,1,0:T(8,128)S(1)} %bitcast.78), channel_id=1, source_target_pairs={{32,0},{64,32},{96,64},{33,1},{65,33},{97,65},{34,2},{66,34},{98,6... | collective-permute-start | bytes 393224 | tf_op jit(solution)/shard_map/ppermute | solution.py:24
  43.3 9.0 %collective-permute-start.5 = (f32[4,2,1,32,128]{4,3,2,1,0:T(8,128)S(1)}, f32[4,2,1,32,128]{4,3,2,1,0:T(8,128)S(1)}, u32[]{:S(2)}, u32[]{:S(2)}) collective-permute-start(f32[4,2,1,32,128]{4,3,2,1,0:T(8,128)S(1)} %bitcast.77), channel_id=1, source_target_pairs={{0,32},{32,64},{64,96},{1,33},{33,65},{65,97},{2,34},{34,66},{66,9... | collective-permute-start | bytes 393224 | tf_op jit(solution)/shard_map/ppermute | solution.py:22
  52.4 6.5 %collective-permute-start.7 = (f32[4,2,50,1,128]{4,2,3,1,0:T(8,128)S(1)}, f32[4,2,50,1,128]{4,2,3,1,0:T(8,128)S(1)}, u32[]{:S(2)}, u32[]{:S(2)}) collective-permute-start(f32[4,2,50,1,128]{4,2,3,1,0:T(8,128)S(1)} %get-tuple-element.19), channel_id=1, source_target_pairs={{0,1},{1,2},{2,3},{4,5},{5,6},{6,7},{8,9},{9,10},{10,11},{12,13},{... | collective-permute-start | bytes 614408 | tf_op jit(solution)/shard_map/ppermute | solution.py:22
  56.0 6.8 %collective-permute-start.6 = (f32[4,2,50,1,128]{4,2,3,1,0:T(8,128)S(1)}, f32[4,2,50,1,128]{4,2,3,1,0:T(8,128)S(1)}, u32[]{:S(2)}, u32[]{:S(2)}) collective-permute-start(f32[4,2,50,1,128]{4,2,3,1,0:T(8,128)S(1)} %get-tuple-element.18), channel_id=1, source_target_pairs={{1,0},{2,1},{3,2},{5,4},{6,5},{7,6},{9,8},{10,9},{11,10},{13,12},{... | collective-permute-start | bytes 614408 | tf_op jit(solution)/shard_map/ppermute | solution.py:24
  62.8 10.0 %copy-start.7 = (f32[4]{0:T(128)S(1)}, f32[4]{0:T(128)}, u32[]{:S(2)}) copy-start(f32[4]{0:T(128)} %param.5) | copy-start | bytes 52
  148.9 147.8 %reduce-scatter.6.cloned.1.call-start = ((), (), s32[]{:S(2)}) async-start(), calls=%async_computation.4 | async-start | bytes 1671168 | tf_op jit(solution)/shard_map/reduce_scatter | solution.py:69
  226.9 171.2 %reduce-scatter.8.cloned.1.call-start = ((), (), s32[]{:S(2)}) async-start(), calls=%async_computation.5 | async-start | bytes 1671168 | tf_op jit(solution)/shard_map/reduce_scatter | solution.py:69
  467.8 4.6 copy-start.3
  472.4 2.7 copy-start
  476.0 11.4 %collective-permute-start.8 = (f32[4,2,1,32,128]{4,3,2,1,0:T(8,128)}, f32[4,2,1,32,128]{4,3,2,1,0:T(8,128)S(1)}, u32[]{:S(2)}, u32[]{:S(2)}) collective-permute-start(f32[4,2,1,32,128]{4,3,2,1,0:T(8,128)} %bitcast.17), channel_id=1, source_target_pairs={{32,0},{64,32},{96,64},{33,1},{65,33},{97,65},{34,2},{66,34},{98,6... | collective-permute-start | bytes 393224 | tf_op jit(solution)/shard_map/ppermute | solution.py:24
  482.7 5.6 %collective-permute-start.9 = (f32[4,2,1,32,128]{4,3,2,1,0:T(8,128)S(1)}, f32[4,2,1,32,128]{4,3,2,1,0:T(8,128)S(1)}, u32[]{:S(2)}, u32[]{:S(2)}) collective-permute-start(f32[4,2,1,32,128]{4,3,2,1,0:T(8,128)S(1)} %bitcast.76), channel_id=1, source_target_pairs={{0,32},{32,64},{64,96},{1,33},{33,65},{65,97},{2,34},{34,66},{66,9... | collective-permute-start | bytes 393224 | tf_op jit(solution)/shard_map/ppermute | solution.py:22
  486.5 7.7 %copy-start.1 = (f32[4,2,48,32,128]{4,2,3,1,0:T(8,128)S(1)}, f32[4,2,48,32,128]{4,2,3,1,0:T(8,128)}, u32[]{:S(2)}) copy-start(f32[4,2,48,32,128]{4,2,3,1,0:T(8,128)} %copy-done) | copy-start | bytes 18874372
  490.3 10.7 %collective-permute-start.11 = (f32[4,2,50,1,128]{4,2,3,1,0:T(8,128)}, f32[4,2,50,1,128]{4,2,3,1,0:T(8,128)}, u32[]{:S(2)}, u32[]{:S(2)}) collective-permute-start(f32[4,2,50,1,128]{4,2,3,1,0:T(8,128)} %get-tuple-element.17), channel_id=1, source_target_pairs={{0,1},{1,2},{2,3},{4,5},{5,6},{6,7},{8,9},{9,10},{10,11},{12,13},{... | collective-permute-start | bytes 614408 | tf_op jit(solution)/shard_map/ppermute | solution.py:22
  492.8 4.8 copy-start.4
  492.8 8.2 %collective-permute-start.10 = (f32[4,2,50,1,128]{4,2,3,1,0:T(8,128)}, f32[4,2,50,1,128]{4,2,3,1,0:T(8,128)}, u32[]{:S(2)}, u32[]{:S(2)}) collective-permute-start(f32[4,2,50,1,128]{4,2,3,1,0:T(8,128)} %get-tuple-element.16), channel_id=1, source_target_pairs={{1,0},{2,1},{3,2},{5,4},{6,5},{7,6},{9,8},{10,9},{11,10},{13,12},{... | collective-permute-start | bytes 614408 | tf_op jit(solution)/shard_map/ppermute | solution.py:24
Sparse Core Ops, SparseCore 0:
  149.0 47.1 reduce-scatter.3
  227.0 69.5 reduce-scatter.5
  330.1 68.0 reduce-scatter.7
where the time goes:
time: 546 us; the launch traced here: 537 us
  waiting for transfers between devices  198 us (36%)
  blocking collectives  128 us (23%)
  other arithmetic  65.3 us (12%)
  local copies, waits for them, and re-layouts  63.3 us (12%)
  starting transfers between devices  41.6 us (8%)
  matrix products  25.4 us (5%)
  between operations  15.2 us (3%)
    reduce_scatter x2, waiting for transfers between devices, plane_sine(): lax.psum_scatter(row_blocks, ('slab', 'pois'), scatter_dimension=0, tiled...  136 us
    psum x1, blocking collectives, body(): total = lax.psum(jnp.sum(density_part), ('slab', 'orb', 'pois'))  67.3 us
    all_gather x1, blocking collectives, body(): section = lax.all_gather(field_part, 'orb', axis=2, tiled=True)  60.6 us
    reduce_scatter x1, waiting for transfers between devices, body(): lax.psum_scatter(jnp.einsum('cz,xyz->cxy', sines, density_part, precision...  47.2 us
    sub x2, other arithmetic, taylor_step(): center + time_step * rotated - 0.5 * time_step * time_step * image_two  34.1 us
    ppermute x6, starting transfers between devices, extended(): lax.ppermute(tail, axis, [(i, (i + 1) % count) for i in range(ends)])  25.2 us
    ppermute x6, starting transfers between devices, extended(): lax.ppermute(head, axis, [((i + 1) % count, i) for i in range(ends)])  16.1 us
    sub x2, other arithmetic, hamiltonian(): return (3.0 + potential) * center - 0.5 * beside_all  15.3 us
  transfers between devices with their start and end apart: 15, of which 12 were waited for; matrix products, arithmetic and copies ran while one was open for 2% of the time, Pallas kernels for 0%

commit v1 on v0

v1 whole, which is shorter than its diff:
```python
import functools
import math

import jax
import jax.numpy as jnp
import numpy as np
from jax import lax
from jax.experimental import pallas as pl
from jax.experimental.pallas import tpu as pltpu
from jax.sharding import PartitionSpec as P

NX, NY, NZ = 192, 128, 128
SLABS, ORBS, POIS = 4, 8, 4
WX, WY = NX // SLABS, NY // POIS
COMPS = 8
FWD = 13
BACK = 14
DEVICES = SLABS * ORBS * POIS
TRANSPOSE_AXES = ("orb", "pois", "slab")
DT = 0.3
HIGHEST = lax.Precision.HIGHEST
VMEM_LIMIT = 40 * 1024 * 1024
f32, bf16 = jnp.float32, jnp.bfloat16


def _sines(n):
    k = np.arange(1, n + 1)
    return np.sin(np.pi * ((k[:, None] * k[None, :]) % (2 * (n + 1))) / (n + 1))


def _lam(n):
    return 2.0 - 2.0 * np.cos(np.pi * np.arange(1, n + 1) / (n + 1))


@functools.cache
def _tables():
    sx, sy = _sines(NX), _sines(NY)
    order = np.array([s * WX + 4 * xb + xi for xi in range(4) for s in range(SLABS) for xb in range(WX // 4)])
    padded = np.zeros((SLABS * 64, NX))
    for s in range(SLABS):
        padded[s * 64 : s * 64 + WX] = sx[s * WX : (s + 1) * WX]
    ring_x = np.zeros((16, NX))
    ring_y = np.zeros((16, NY))
    for s in range(SLABS):
        if s > 0:
            ring_x[s] = sx[s * WX - 1]
        if s < SLABS - 1:
            ring_x[8 + s] = sx[(s + 1) * WX]
    for p in range(POIS):
        if p > 0:
            ring_y[p] = sy[p * WY - 1]
        if p < POIS - 1:
            ring_y[8 + p] = sy[(p + 1) * WY]
    back_x = np.concatenate([sx[order], padded, ring_x])
    modes = np.stack([_lam(NZ), sy.sum(1)])
    cast = lambda a: np.asarray(a, np.float32)
    return dict(
        sy=cast(sy),
        forward_x=cast(sx[:, order]),
        back_x=cast(back_x),
        ring_y=cast(ring_y),
        col=cast(np.stack([_lam(NX), sx.sum(1)] + [np.zeros(NX)] * 6, 1)),
        row=cast(np.stack([_lam(NY), sy.sum(1)] + [np.zeros(NY)] * 6, 0)),
        modes=cast(modes),
    )


def _iotas():
    return (
        lax.broadcasted_iota(jnp.int32, (8, 128), 0),
        lax.broadcasted_iota(jnp.int32, (8, 128), 1),
    )


def _zsum(v, lane):
    return jnp.where(lane == 0, 0.0, pltpu.roll(v, 1, 1)) + jnp.where(lane == 127, 0.0, pltpu.roll(v, 127, 1))


def _beside(below, v, above, low_row, high_row, sub, lane):
    down = [pltpu.roll(a, 1, 0) for a in v]
    up = [pltpu.roll(a, 7, 0) for a in v]
    out = []
    for i in range(4):
        d = jnp.where(sub == 0, down[i - 1] if i else low_row, down[i])
        u = jnp.where(sub == 7, up[i + 1] if i < 3 else high_row, up[i])
        out.append(((below[i] + above[i]) + (d + u)) + _zsum(v[i], lane))
    return out


def _pieces(plane):
    return [plane[8 * i : 8 * i + 8] for i in range(4)]


def _row8(ref_row):
    return jnp.broadcast_to(ref_row, (8, 128))


def _faces_kernel(psi, ext, old, x_left, x_right, y_left, y_right, c_ll, c_lr, c_rl, c_rr, rows):
    step = pl.program_id(0)

    @pl.when(step < COMPS)
    def _():
        x_left[0] = psi[0, 0:2]
        x_right[0] = psi[0, WX - 2 : WX]

        def fill(x, carry):
            top = psi[0, x, 0:16, :].astype(f32)
            bottom = psi[0, x, 16:32, :].astype(f32)
            rows[0, pl.ds(8 * x, 8), :] = top[0:8]
            rows[1, pl.ds(8 * x, 8), :] = bottom[8:16]
            return carry

        lax.fori_loop(0, WX, fill, 0, unroll=8)
        for half, ref, first in ((0, y_left, 0), (1, y_right, 6)):
            for d in range(2):
                ref[0, d] = rows[half, pl.ds(first + d, WX, 8), :].astype(bf16)
        for ref, half, y, x in (
            (c_ll, 0, 0, 0),
            (c_lr, 1, 7, 0),
            (c_rl, 0, 0, WX - 1),
            (c_rr, 1, 7, WX - 1),
        ):
            ref[0] = jnp.broadcast_to(rows[half, pl.ds(8 * x + y, 1), :], (8, 128)).astype(bf16)

    def potential(ref):
        def split(value, out, slot):
            high = value.astype(bf16)
            out[0, slot] = high
            out[0, slot + 1] = (value - high.astype(f32)).astype(bf16)

        split(ref[0], x_left, 0)
        split(ref[WX - 1], x_right, 0)

        def fill(x, carry):
            rows[0, pl.ds(8 * x, 8), :] = ref[x, 0:8, :]
            rows[1, pl.ds(8 * x, 8), :] = ref[x, 24:32, :]
            return carry

        lax.fori_loop(0, WX, fill, 0, unroll=8)
        split(rows[0, pl.ds(0, WX, 8), :], y_left, 0)
        split(rows[1, pl.ds(7, WX, 8), :], y_right, 0)
        for ref_c in (c_ll, c_lr, c_rl, c_rr):
            ref_c[0] = jnp.zeros((8, 128), bf16)

    @pl.when(step == COMPS)
    def _():
        potential(ext)

    @pl.when(step == COMPS + 1)
    def _():
        potential(old)


def _faces(psi, ext, old):
    steps = COMPS + 2
    whole = pl.BlockSpec((WX, WY, NZ), lambda i: (0, 0, 0))
    block = lambda *dims: pl.BlockSpec((1,) + dims, lambda i: (i,) + (0,) * len(dims))
    x_face, y_face, corner = (2, WY, NZ), (2, WX, NZ), (8, NZ)
    shapes = [x_face, x_face, y_face, y_face] + [corner] * 4
    return pl.pallas_call(
        _faces_kernel,
        name="faces",
        grid=(steps,),
        in_specs=[
            pl.BlockSpec((1, WX, WY, NZ), lambda i: (jnp.minimum(i, COMPS - 1), 0, 0, 0)),
            whole,
            whole,
        ],
        out_specs=[block(*s) for s in shapes],
        out_shape=[jax.ShapeDtypeStruct((steps,) + s, bf16) for s in shapes],
        scratch_shapes=[pltpu.VMEM((2, 8 * WX, 128), f32)],
        cost_estimate=pl.CostEstimate(flops=1000000, bytes_accessed=6000000, transcendentals=0),
    )(psi, ext, old)


def _images(psi, halo, mine, pot, ring, images, face_psi, face_image):
    x_low, x_high, y_low, y_high, corners = halo
    mine_low, mine_high = mine
    ring_y, ring_x = ring
    sub, lane = _iotas()
    slab, pois = lax.axis_index("slab"), lax.axis_index("pois")
    inside = lambda cond: jnp.where(cond, 1.0, 0.0).astype(f32)
    in_x = (inside(slab > 0), inside(slab < SLABS - 1))
    in_y = (inside(pois > 0), inside(pois < POIS - 1))

    def edge(c, carry):
        corner = [[corners[2 * i + j][c].astype(f32) for j in range(2)] for i in range(2)]
        for side, (far, near, own) in enumerate(((y_low, 1, mine_low), (y_high, 0, mine_high))):
            one = far[c, near].astype(f32)
            two = far[c, 1 - near].astype(f32)
            zero = own[c, side].astype(f32)
            n = WX // 8
            cells = [one[8 * i : 8 * i + 8] for i in range(n)]
            down = [pltpu.roll(a, 1, 0) for a in cells]
            up = [pltpu.roll(a, 7, 0) for a in cells]
            for i in range(n):
                d = jnp.where(sub == 0, down[i - 1] if i else corner[0][side], down[i])
                u = jnp.where(sub == 7, up[i + 1] if i < n - 1 else corner[1][side], up[i])
                total = (d + u) + (zero[8 * i : 8 * i + 8] + two[8 * i : 8 * i + 8]) + _zsum(cells[i], lane)
                face_psi[side, c, 8 * i : 8 * i + 8] = cells[i]
                face_image[side, c, 8 * i : 8 * i + 8] = in_y[side] * (
                    ring_y[side, 8 * i : 8 * i + 8] * cells[i] - 0.5 * total
                )
        plane = lambda ref, *i: _pieces(ref[(c,) + i].astype(f32))
        m2, m1 = plane(x_low, 0), plane(x_low, 1)
        q0, q1 = plane(x_high, 0), plane(x_high, 1)
        p0, p1, p46, p47 = plane(psi, 0), plane(psi, 1), plane(psi, WX - 2), plane(psi, WX - 1)
        for x, below, v, above, weight, scale, low, high in (
            (-1, m2, m1, p0, lambda i: ring_x[0, 8 * i : 8 * i + 8], in_x[0], corner[0][0], corner[0][1]),
            (0, m1, p0, p1, lambda i: pot[0, 8 * i : 8 * i + 8], None, 0, 0),
            (WX - 1, p46, p47, q0, lambda i: pot[WX - 1, 8 * i : 8 * i + 8], None, 0, 0),
            (WX, p47, q0, q1, lambda i: ring_x[1, 8 * i : 8 * i + 8], in_x[1], corner[1][0], corner[1][1]),
        ):
            if scale is None:
                low, high = (_row8(face_psi[side, c, x : x + 1, :]) for side in range(2))
            total = _beside(below, v, above, low, high, sub, lane)
            for i in range(4):
                value = weight(i) * v[i] - 0.5 * total[i]
                images[c, x + 1, 8 * i : 8 * i + 8] = value if scale is None else scale * value
        return carry

    lax.fori_loop(0, COMPS, edge, 0)

    def inner(x, carry):
        weight = [pot[x, 8 * i : 8 * i + 8] for i in range(4)]
        for c in range(COMPS):
            below, v, above = (_pieces(psi[c, x + d].astype(f32)) for d in (-1, 0, 1))
            low, high = (_row8(face_psi[side, c, pl.ds(x, 1), :]) for side in range(2))
            total = _beside(below, v, above, low, high, sub, lane)
            for i in range(4):
                images[c, x + 1, 8 * i : 8 * i + 8] = weight[i] * v[i] - 0.5 * total[i]
        return carry

    lax.fori_loop(1, WX - 1, inner, 0)


def _stepped(psi, orbital, x, weight, images, face_image, sub, lane):
    parts = []
    for c in (2 * orbital, 2 * orbital + 1):
        below, u, above = ([images[c, x + d, 8 * i : 8 * i + 8] for i in range(4)] for d in (0, 1, 2))
        low, high = (_row8(face_image[side, c, pl.ds(x, 1), :]) for side in range(2))
        total = _beside(below, u, above, low, high, sub, lane)
        second = [weight[i] * u[i] - 0.5 * total[i] for i in range(4)]
        parts.append((_pieces(psi[c, x].astype(f32)), u, second))
    (a, ua, wa), (b, ub, wb) = parts
    half = 0.5 * DT * DT
    real = [a[i] + DT * ub[i] - half * wa[i] for i in range(4)]
    imag = [b[i] - DT * ua[i] - half * wb[i] for i in range(4)]
    return real, imag


def _charge_kernel(
    occupations, psi, ext, old, x_low, x_high, y_low, y_high, c_ll, c_lr, c_rl, c_rr, mine_low, mine_high, sines,
    message, images, face_psi, face_image, pot, ring_y, ring_x, charge,
):
    sub, lane = _iotas()
    pot[...] = 3.0 + (ext[...] + old[...])
    pair = lambda ref, k: ref[k, 0].astype(f32) + ref[k, 1].astype(f32)
    for side, ref in enumerate((y_low, y_high)):
        ring_y[side] = 3.0 + (pair(ref, COMPS) + pair(ref, COMPS + 1))
    for side, ref in enumerate((x_low, x_high)):
        ring_x[side] = 3.0 + (pair(ref, COMPS) + pair(ref, COMPS + 1))
    _images(
        psi, (x_low, x_high, y_low, y_high, (c_ll, c_lr, c_rl, c_rr)), (mine_low, mine_high), pot, (ring_y, ring_x),
        images, face_psi, face_image,
    )
    occ = [occupations[k] for k in range(COMPS // 2)]

    def group(g, totals):
        def one(xi, carry):
            x = 4 * g + xi
            weight = [pot[x, 8 * i : 8 * i + 8] for i in range(4)]
            sums = [jnp.zeros((8, 128), f32) for _ in range(4)]
            for orbital in range(COMPS // 2):
                real, imag = _stepped(psi, orbital, x, weight, images, face_image, sub, lane)
                sums = [sums[i] + occ[orbital] * (real[i] * real[i] + imag[i] * imag[i]) for i in range(4)]
            for i in range(4):
                charge[pl.ds(pl.multiple_of(32 * xi + 8 * i, 8), 8), :] = sums[i]
            return carry + ((sums[0] + sums[1]) + (sums[2] + sums[3]))

        totals = lax.fori_loop(0, 4, one, totals)
        modes = lax.dot_general(
            sines[...], charge[...], (((1,), (1,)), ((), ())), precision=HIGHEST, preferred_element_type=f32
        )
        for k in range(16):
            message[pl.ds(8 * FWD * k + g, 8, FWD), :] = modes[8 * k : 8 * k + 8]
        return totals

    totals = lax.fori_loop(0, WX // 4, group, jnp.zeros((8, 128), f32))
    totals = jnp.broadcast_to(jnp.sum(totals, axis=0, keepdims=True), (8, 128))
    for k in range(16):
        message[pl.ds(8 * FWD * k + FWD - 1, 8, FWD), :] = totals


_IMAGE_SCRATCH = [
    pltpu.VMEM((COMPS, WX + 2, WY, NZ), f32),
    pltpu.VMEM((2, COMPS, WX, NZ), f32),
    pltpu.VMEM((2, COMPS, WX, NZ), f32),
    pltpu.VMEM((WX, WY, NZ), f32),
    pltpu.VMEM((2, WX, NZ), f32),
    pltpu.VMEM((2, WY, NZ), f32),
]

_VM = pl.BlockSpec(memory_space=pltpu.VMEM)
_SM = pl.BlockSpec(memory_space=pltpu.SMEM)


def _charge_messages(occupations, *arrays):
    return pl.pallas_call(
        _charge_kernel,
        name="charge",
        in_specs=[_SM] + [_VM] * len(arrays),
        out_specs=_VM,
        out_shape=jax.ShapeDtypeStruct((DEVICES * FWD, 128), f32),
        scratch_shapes=_IMAGE_SCRATCH + [pltpu.VMEM((128, 128), f32)],
        compiler_params=pltpu.CompilerParams(vmem_limit_bytes=VMEM_LIMIT),
        cost_estimate=pl.CostEstimate(flops=100000000, bytes_accessed=8000000, transcendentals=0),
    )(occupations, *arrays)


def _swap_groups(blocks, group):
    out = []
    for i in range(4):
        value = None
        for j in range(4):
            shift = (32 * (j - i)) % 128
            moved = pltpu.roll(blocks[j], shift, 1) if shift else blocks[j]
            value = moved if value is None else jnp.where(group == j, moved, value)
        out.append(value)
    return out


def _plane_kernel(modes, recv, forward_x, sy, back_x, ring_y, col, row, send, packed, block):
    dot = functools.partial(jnp.dot, precision=HIGHEST, preferred_element_type=f32)
    nt = lambda a, b: lax.dot_general(a, b, (((1,), (1,)), ((), ())), precision=HIGHEST, preferred_element_type=f32)
    kz = (lax.axis_index("orb") * POIS + lax.axis_index("pois")) * SLABS + lax.axis_index("slab")
    lam_z, sum_z = modes[0, kz], modes[1, kz]
    for p in range(POIS):
        for s in range(SLABS):
            total = None
            for o in range(ORBS):
                part = recv[pl.ds(((o * POIS + p) * SLABS + s) * FWD, 12), :]
                total = part if total is None else total + part
            packed[p, pl.ds(12 * s, 12), :] = total
    charge_total = jnp.sum(recv[pl.ds(FWD - 1, DEVICES, FWD), :])
    mean = charge_total / (NX * NY * NZ)
    group = lax.broadcasted_iota(jnp.int32, (WX, 128), 1) // 32
    plane = jnp.concatenate(_swap_groups([packed[p] for p in range(POIS)], group), axis=0)
    spectrum = dot(dot(forward_x[...], plane), sy[...])
    uniform = (mean * sum_z) * (col[:, 1:2] * row[1:2, :])
    divisor = col[:, 0:1] + row[0:1, :] + lam_z
    factor = 32.0 * math.pi / ((NX + 1) * (NY + 1) * (NZ + 1))
    scaled = (spectrum - uniform) * factor / divisor
    across = dot(back_x[...], scaled)
    field = dot(across[:NX], sy[...])
    ring = dot(across[NX + 256 :], sy[...])
    cells = _swap_groups([field[WX * i : WX * (i + 1)] for i in range(4)], group)
    lane8 = lax.broadcasted_iota(jnp.int32, (8, 128), 1)
    group8 = lane8 // 32
    faces = [nt(ring_y[...], across[NX + 128 * h : NX + 128 * (h + 1)]) for h in range(2)]
    y_rows = []
    for s in range(SLABS):
        low, high = faces[s // 2][0:8], faces[s // 2][8:16]
        if s % 2 == 0:
            high = pltpu.roll(high, 64, 1)
        else:
            low = pltpu.roll(low, 64, 1)
        y_rows.append(jnp.where(lane8 < 64, low, high))
    for p in range(POIS):
        shift = lambda v, k: pltpu.roll(v, k % 128, 1) if k % 128 else v
        x_rows = jnp.where(
            group8 == 0,
            shift(ring[0:8], -32 * p),
            jnp.where(group8 == 1, shift(ring[8:16], 32 - 32 * p), 0.0),
        )
        for s in range(SLABS):
            base = (p * SLABS + s) * BACK
            block[pl.ds(base, 12), :] = cells[p][12 * s : 12 * s + 12]
            block[pl.ds(base + 12, 1), :] = x_rows[s : s + 1]
            block[pl.ds(base + 13, 1), :] = y_rows[s][p : p + 1]
    count = POIS * SLABS * BACK
    for o in range(ORBS):
        send[pl.ds(o * count, count), :] = block[...]


def _plane(recv):
    t = _tables()
    return pl.pallas_call(
        _plane_kernel,
        name="plane",
        in_specs=[_SM] + [_VM] * 7,
        out_specs=_VM,
        out_shape=jax.ShapeDtypeStruct((DEVICES * BACK, 128), f32),
        scratch_shapes=[
            pltpu.VMEM((POIS, WX, 128), f32),
            pltpu.VMEM((POIS * SLABS * BACK, 128), f32),
        ],
        cost_estimate=pl.CostEstimate(flops=200000000, bytes_accessed=3000000, transcendentals=0),
    )(
        jnp.asarray(t["modes"]),
        recv,
        *(jnp.asarray(t[k]) for k in ("forward_x", "sy", "back_x", "ring_y", "col", "row")),
    )


def _step_kernel(
    psi, ext, old, x_low, x_high, y_low, y_high, c_ll, c_lr, c_rl, c_rr, mine_low, mine_high, sines, recv,
    new, hartree, images, face_psi, face_image, pot, ring_y, ring_x,
):
    sub, lane = _iotas()
    orb = lax.axis_index("orb")
    back = lambda r: lax.dot_general(
        recv[pl.ds(r, 128, BACK), :], sines[...], (((0,), (0,)), ((), ())), precision=HIGHEST, preferred_element_type=f32
    )
    shift = lax.rem(128 - 16 * orb, 128)

    def planes(g, carry):
        field = back(g)
        mine = pltpu.roll(field, shift, 1)
        for xi in range(4):
            x = 4 * g + xi
            cells = field[32 * xi : 32 * xi + 32]
            pot[x] = 3.0 + (ext[x] + 0.5 * (old[x] + cells))
            hartree[x] = mine[32 * xi : 32 * xi + 32, 0:16]
        return carry

    lax.fori_loop(0, WX // 4, planes, 0)
    pair = lambda ref, k: ref[k, 0].astype(f32) + ref[k, 1].astype(f32)
    field = back(12)
    for side, ref in enumerate((x_low, x_high)):
        cells = field[32 * side : 32 * side + 32]
        ring_x[side] = 3.0 + (pair(ref, COMPS) + 0.5 * (pair(ref, COMPS + 1) + cells))
    field = back(13)
    for side, ref in enumerate((y_low, y_high)):
        cells = field[64 * side : 64 * side + WX]
        ring_y[side] = 3.0 + (pair(ref, COMPS) + 0.5 * (pair(ref, COMPS + 1) + cells))
    _images(
        psi, (x_low, x_high, y_low, y_high, (c_ll, c_lr, c_rl, c_rr)), (mine_low, mine_high), pot, (ring_y, ring_x),
        images, face_psi, face_image,
    )

    def one(x, carry):
        weight = [pot[x, 8 * i : 8 * i + 8] for i in range(4)]
        for orbital in range(COMPS // 2):
            real, imag = _stepped(psi, orbital, x, weight, images, face_image, sub, lane)
            for i in range(4):
                new[2 * orbital, x, 8 * i : 8 * i + 8] = real[i]
                new[2 * orbital + 1, x, 8 * i : 8 * i + 8] = imag[i]
        return carry

    lax.fori_loop(0, WX, one, 0)


def _step(*arrays):
    return pl.pallas_call(
        _step_kernel,
        name="step",
        in_specs=[_VM] * len(arrays),
        out_specs=[_VM, _VM],
        out_shape=[
            jax.ShapeDtypeStruct((COMPS, WX, WY, NZ), f32),
            jax.ShapeDtypeStruct((WX, WY, NZ // ORBS), f32),
        ],
        scratch_shapes=_IMAGE_SCRATCH,
        compiler_params=pltpu.CompilerParams(vmem_limit_bytes=VMEM_LIMIT),
        cost_estimate=pl.CostEstimate(flops=100000000, bytes_accessed=12000000, transcendentals=0),
    )(*arrays)


def _exchange(sent):
    x_left, x_right, y_left, y_right, c_ll, c_lr, c_rl, c_rr = sent
    up = lambda n: [(i, i + 1) for i in range(n - 1)]
    down = lambda n: [(i + 1, i) for i in range(n - 1)]
    y_low = lax.ppermute(y_right, "pois", up(POIS))
    y_high = lax.ppermute(y_left, "pois", down(POIS))
    x_low = lax.ppermute(x_right, "slab", up(SLABS))
    x_high = lax.ppermute(x_left, "slab", down(SLABS))

    def diagonal(value, ds, dp):
        pairs = [
            (s * POIS + p, (s + ds) * POIS + p + dp)
            for s in range(SLABS)
            for p in range(POIS)
            if 0 <= s + ds < SLABS and 0 <= p + dp < POIS
        ]
        return lax.ppermute(value, ("slab", "pois"), pairs)

    return (
        x_low, x_high, y_low, y_high,
        diagonal(c_rr, 1, 1), diagonal(c_rl, 1, -1), diagonal(c_lr, -1, 1), diagonal(c_ll, -1, -1),
        y_left, y_right,
    )


def _swap(messages, rows):
    moved = lax.all_to_all(messages.reshape(DEVICES, 1, rows * 128), TRANSPOSE_AXES, 0, 0)
    return moved.reshape(DEVICES * rows, 128)


def body(orbitals, occupations, ext_pot, hartree_old):
    psi = orbitals.reshape(COMPS, WX, WY, NZ)
    halo = _exchange(_faces(psi, ext_pot, hartree_old))
    sines = jnp.asarray(_tables()["sy"])
    message = _charge_messages(occupations, psi, ext_pot, hartree_old, *halo, sines)
    back = _swap(_plane(_swap(message, FWD)), BACK)
    new, hartree = _step(psi, ext_pot, hartree_old, *halo, sines, back)
    return new.reshape(orbitals.shape), hartree


def solution(mesh):
    placed = (P("orb", None, "slab", "pois", None), P("orb"), P("slab", "pois", None), P("slab", "pois", None))
    return jax.shard_map(
        body,
        mesh=mesh,
        in_specs=placed,
        out_specs=(P("orb", None, "slab", "pois", None), P("slab", "pois", "orb")),
        check_vma=False,
    )
```

time: 546 us -> 160 us (0.29); the launches traced: 537 us -> 159 us
  waiting for transfers between devices: 198 us -> 17.9 us
  blocking collectives: 128 us -> 47.4 us
  other arithmetic: 65.3 us -> 0 us
  Pallas kernels: 0 us -> 49 us
  local copies, waits for them, and re-layouts: 63.3 us -> 18.7 us
  matrix products: 25.4 us -> 0 us
  starting transfers between devices: 41.6 us -> 24.9 us
  between operations: 15.2 us -> 0.82 us
    reduce_scatter x3 -> x0, waiting for transfers between devices: 183 us -> none  [the longest x2 136 us: plane_sine(): lax.psum_scatter(row_blocks, ('slab', 'pois'), scatter_dimension=0, tiled...]
    psum x1 -> x0, blocking collectives: 67.3 us -> none  [body(): total = lax.psum(jnp.sum(density_part), ('slab', 'orb', 'pois'))]
    all_gather x1 -> x0, blocking collectives: 60.6 us -> none  [body(): section = lax.all_gather(field_part, 'orb', axis=2, tiled=True)]
    sub x8 -> x0, other arithmetic: 51.5 us -> none  [the longest x2 34.1 us: taylor_step(): center + time_step * rotated - 0.5 * time_step * time_step * image_two]
    pallas_call x0 -> x4, Pallas kernels: none -> 49 us  [the longest x1 20 us: _step(): pl.pallas_call(_step_kernel, name='step', in_specs=[_VM] * len(arrays), o...]
    all_to_all x0 -> x2, blocking collectives: none -> 47.4 us  [_swap(): lax.all_to_all(messages.reshape(DEVICES, 1, rows * 128), TRANSPOSE_AXES,...]
    transpose x6 -> x0, local copies, waits for them, and re-layouts: 26.1 us -> none  [the longest x2 14.1 us: plane_sine(): row_blocks = jnp.transpose(row_blocks, (0, 2, 1, 3, 4)).reshape(-1, width_c)]
    dot_general x6 -> x0, matrix products: 25.4 us -> none  [the longest x2 8.13 us: plane_sine(): jnp.einsum('by,ayc->abc', sines_y, partial_sum, precision=highest)]
  transfers between devices with their start and end apart: 15 -> 8, of which waited for: 12 -> 4; matrix products, arithmetic and copies ran while one was open for 2% -> 0% of each run, Pallas kernels for 0% -> 0%
where the time goes in v1:
time: 160 us; the launch traced here: 159 us
  Pallas kernels  49 us (31%)
  blocking collectives  47.4 us (30%)
  starting transfers between devices  24.9 us (16%)
  local copies, waits for them, and re-layouts  18.7 us (12%)
  waiting for transfers between devices  17.9 us (11%)
    all_to_all x2, blocking collectives, _swap(): lax.all_to_all(messages.reshape(DEVICES, 1, rows * 128), TRANSPOSE_AXES,...  47.4 us
    pallas_call x1, Pallas kernels, _step(): pl.pallas_call(_step_kernel, name='step', in_specs=[_VM] * len(arrays), o...  20 us
    unnamed x55, local copies, waits for them, and re-layouts  18.7 us
    ppermute x4, waiting for transfers between devices, diagonal(): return lax.ppermute(value, ('slab', 'pois'), pairs)  17.9 us
    pallas_call x1, Pallas kernels, _charge_messages(): pl.pallas_call(_charge_kernel, name='charge', in_specs=[_SM] + [_VM] * le...  17 us
    ppermute x4, starting transfers between devices, diagonal(): return lax.ppermute(value, ('slab', 'pois'), pairs)  11.7 us
    pallas_call x1, Pallas kernels, _faces(): pl.pallas_call(_faces_kernel, name='faces', grid=(steps,), in_specs=[pl.B...  7.11 us
    ppermute x1, starting transfers between devices, _exchange(): x_low = lax.ppermute(x_right, 'slab', up(SLABS))  5.66 us
  transfers between devices with their start and end apart: 8, of which 4 were waited for; matrix products, arithmetic and copies ran while one was open for 0% of the time, Pallas kernels for 0%

profile of v1, /device:TPU:1, one launch (start us, length us, event | category | flops | bytes accessed | tf_op | source)
XLA Modules:
  0.0 158.7 jit_solution(1963452152447676533)
XLA Ops:
  0.6 0.0 copy-start
  0.6 7.1 %faces.1 = (bf16[10,2,32,128]{3,2,1,0:T(8,128)(2,1)}, bf16[10,2,32,128]{3,2,1,0:T(8,128)(2,1)}, bf16[10,2,48,128]{3,2,1,0:T(8,128)(2,1)}, bf16[10,2,48,128]{3,2,...) custom-call(bf16[8,48,32,128]{3,2,1,0:T(8,128)(2,1)} %bitcast.6, ...), custom_call_target="tpu_custom_call" | custom-call | flops 1000000 | bytes 6000000 | tf_op jit(solution)/shard_map/faces/pallas_call | solution.py:160
  7.8 4.4 %collective-permute-start.2 = (bf16[10,2,48,128]{3,2,1,0:T(8,128)(2,1)}, bf16[10,2,48,128]{3,2,1,0:T(8,128)(2,1)S(1)}, u32[]{:S(2)}, u32[]{:S(2)}) collective-permute-start(bf16[10,2,48,128]{3,2,1,0:T(8,128)(2,1)} %get-tuple-element.14.mine_high), channel_id=1, source_target_pairs={{0,1},{1,2},{2,3},{4,5},{5,6},{6,7},{8,9},{9,10},{10,11},{12,13},{... | collective-permute-start | bytes 737288 | tf_op jit(solution)/shard_map/ppermute | solution.py:474
  12.1 1.3 collective-permute-start.3
  13.4 5.7 %collective-permute-start = (bf16[10,2,32,128]{3,2,1,0:T(8,128)(2,1)}, bf16[10,2,32,128]{3,2,1,0:T(8,128)(2,1)S(1)}, u32[]{:S(2)}, u32[]{:S(2)}) collective-permute-start(bf16[10,2,32,128]{3,2,1,0:T(8,128)(2,1)} %get-tuple-element.12), channel_id=1, source_target_pairs={{0,32},{32,64},{64,96},{1,33},{33,65},{65,97},{2,34},{34,66},{66,9... | collective-permute-start | bytes 491528 | tf_op jit(solution)/shard_map/ppermute | solution.py:476
  19.1 1.9 %collective-permute-start.1 = (bf16[10,2,32,128]{3,2,1,0:T(8,128)(2,1)}, bf16[10,2,32,128]{3,2,1,0:T(8,128)(2,1)S(1)}, u32[]{:S(2)}, u32[]{:S(2)}) collective-permute-start(bf16[10,2,32,128]{3,2,1,0:T(8,128)(2,1)} %get-tuple-element.13), channel_id=1, source_target_pairs={{32,0},{64,32},{96,64},{33,1},{65,33},{97,65},{34,2},{66,34},{98,6... | collective-permute-start | bytes 491528 | tf_op jit(solution)/shard_map/ppermute | solution.py:477
  21.0 7.2 %collective-permute-start.4 = (bf16[10,8,128]{2,1,0:T(8,128)(2,1)}, bf16[10,8,128]{2,1,0:T(8,128)(2,1)S(1)}, u32[]{:S(2)}, u32[]{:S(2)}) collective-permute-start(bf16[10,8,128]{2,1,0:T(8,128)(2,1)} %get-tuple-element.16), channel_id=1, source_target_pairs={{0,33},{1,34},{2,35},{32,65},{33,66},{34,67},{64,97},{65,98},{66,9... | collective-permute-start | bytes 61448 | tf_op jit(solution)/shard_map/ppermute | solution.py:486
  28.3 1.1 collective-permute-done.4.c_ll
  29.4 1.3 collective-permute-start.5
  30.7 4.0 %collective-permute-done.5.c_lr = bf16[10,8,128]{2,1,0:T(8,128)(2,1)S(1)} collective-permute-done((bf16[10,8,128]{2,1,0:T(8,128)(2,1)}, bf16[10,8,128]{2,1,0:T(8,128)(2,1)S(1)}, u32[]{:S(2)}, u32[]{:S(2)}) %collective-permute-start.5) | collective-permute-done | bytes 20512 | tf_op jit(solution)/shard_map/ppermute | solution.py:486
  34.7 1.9 %collective-permute-start.6 = (bf16[10,8,128]{2,1,0:T(8,128)(2,1)}, bf16[10,8,128]{2,1,0:T(8,128)(2,1)S(1)}, u32[]{:S(2)}, u32[]{:S(2)}) collective-permute-start(bf16[10,8,128]{2,1,0:T(8,128)(2,1)} %get-tuple-element.18), channel_id=1, source_target_pairs={{32,1},{33,2},{34,3},{64,33},{65,34},{66,35},{96,65},{97,66},{98,6... | collective-permute-start | bytes 61448 | tf_op jit(solution)/shard_map/ppermute | solution.py:486
  36.6 1.1 collective-permute-done.6.c_rl
  37.7 1.3 collective-permute-start.7
  39.0 11.7 %collective-permute-done.7.c_rr = bf16[10,8,128]{2,1,0:T(8,128)(2,1)S(1)} collective-permute-done((bf16[10,8,128]{2,1,0:T(8,128)(2,1)}, bf16[10,8,128]{2,1,0:T(8,128)(2,1)S(1)}, u32[]{:S(2)}, u32[]{:S(2)}) %collective-permute-start.7) | collective-permute-done | bytes 20512 | tf_op jit(solution)/shard_map/ppermute | solution.py:486
  50.6 0.0 collective-permute-done.x_low
  50.6 0.0 collective-permute-done.1.x_high
  50.7 0.0 copy-start.14
  50.7 0.0 collective-permute-done.2.y_low
  50.7 0.0 collective-permute-done.3.y_high
  50.7 0.0 copy-start.1
  50.7 1.2 copy-done.1
  52.0 1.1 copy-done.3
  53.1 0.9 copy-done.5
  54.0 0.9 copy-done.7
  55.0 0.8 copy-done.16
  55.8 0.7 copy-done.26
  56.5 17.0 %charge.1 = f32[1664,128]{1,0:T(8,128)S(1)} custom-call(f32[4]{0:T(128)S(1)} %copy-done.26, bf16[8,48,32,128]{3,2,1,0:T(8,128)(2,1)S(1)} %bitcast.7, f32[48,32,128]{2,1,0:T(8,128)S(1)} %copy-done.1, f32[48,32,128]{2,1,0:T(8,128)S(1)} %copy-done.3, bf16[10,2,32,128]{3,2,1,0:T(8,128)(2,1)S(1)} %collective-permute-done.x_low, ...), custom_call_target="tpu_custom_call" | custom-call | flops 100000000 | bytes 8000000 | tf_op jit(solution)/shard_map/charge/pallas_call | solution.py:309
  73.4 24.9 %all_to_all.10 = f32[128,1,1664]{2,1,0:T(1,128)} all-to-all(f32[128,1,1664]{2,1,0:T(1,128)S(1)} %bitcast.10), channel_id=1, replica_groups=mesh['slab'=4,'orb'=8,'pois'=4] {'orb','pois','slab'}, dimensions={0} | all-to-all | bytes 1703936 | tf_op jit(solution)/shard_map/all_to_all | solution.py:496
  98.4 0.0 copy-done.24
  98.4 0.0 copy-done.14
  98.4 0.0 copy-done.9
  98.4 0.0 copy-done.11
  98.4 4.9 %plane.1 = f32[1792,128]{1,0:T(8,128)} custom-call(f32[2,128]{1,0:T(2,128)} %constant.15.clone.modes, f32[1664,128]{1,0:T(8,128)} %bitcast.12, f32[192,192]{1,0:T(8,128)} %constant.16.clone.forward_x, f32[128,128]{1,0:T(8,128)} %constant.14.clone.sines.sy, f32[464,192]{1,0:T(8,128)} %constant.17.clone.back_x, f32[16,128]{1,0:T(8,128)} %constant.18.clone.ring_y, ...), custom_call_target="tpu_custom_call" | custom-call | flops 200000000 | bytes 3000000 | tf_op jit(solution)/shard_map/plane/pallas_call | solution.py:388
  103.3 22.5 %all_to_all.11 = f32[128,1,1792]{2,1,0:T(1,128)S(1)} all-to-all(f32[128,1,1792]{2,1,0:T(1,128)} %bitcast.11), channel_id=1, replica_groups=mesh['slab'=4,'orb'=8,'pois'=4] {'orb','pois','slab'}, dimensions={0} | all-to-all | bytes 1835008 | tf_op jit(solution)/shard_map/all_to_all | solution.py:496
  125.8 1.1 copy-done.2
  126.9 1.1 copy-done.4
  128.1 0.9 copy-done.8
  129.0 0.9 copy-done.10
  129.9 0.9 copy-done.12
  130.9 0.9 copy-done.15
  131.8 0.8 copy-done.17
  132.6 0.7 copy-done.19
  133.4 0.7 copy-done.21
  134.1 0.7 copy-done.23
  134.8 0.7 copy-done.25
  135.6 20.0 %step.1 = (f32[8,48,32,128]{3,2,1,0:T(8,128)}, f32[48,32,16]{2,1,0:T(8,128)S(1)}) custom-call(bf16[8,48,32,128]{3,2,1,0:T(8,128)(2,1)S(1)} %bitcast.8, f32[48,32,128]{2,1,0:T(8,128)S(1)} %copy-done.2, f32[48,32,128]{2,1,0:T(8,128)S(1)} %copy-done.4, bf16[10,2,32,128]{3,2,1,0:T(8,128)(2,1)S(1)} %collective-permute-done.x_low, ...), custom_call_target="tpu_custom_call" | custom-call | flops 100000000 | bytes 12000000 | tf_op jit(solution)/shard_map/step/pallas_call | solution.py:455
  155.6 0.9 copy-done.13
  156.5 2.2 %copy.16 = f32[48,32,16]{0,2,1:T(8,128)} copy(f32[48,32,16]{2,1,0:T(8,128)} %copy-done.13) | data formatting | bytes 196608
  (29 shorter events, 0.0 us)
Async XLA Ops:
  0.6 50.1 %copy-start = (bf16[4,2,48,32,128]{4,3,2,1,0:T(8,128)(2,1)S(1)}, bf16[4,2,48,32,128]{4,3,2,1,0:T(8,128)(2,1)}, u32[]{:S(2)}) copy-start(bf16[4,2,48,32,128]{4,3,2,1,0:T(8,128)(2,1)} %param.11) | copy-start | bytes 9437188
  7.8 42.9 %collective-permute-start.2 = (bf16[10,2,48,128]{3,2,1,0:T(8,128)(2,1)}, bf16[10,2,48,128]{3,2,1,0:T(8,128)(2,1)S(1)}, u32[]{:S(2)}, u32[]{:S(2)}) collective-permute-start(bf16[10,2,48,128]{3,2,1,0:T(8,128)(2,1)} %get-tuple-element.14.mine_high), channel_id=1, source_target_pairs={{0,1},{1,2},{2,3},{4,5},{5,6},{6,7},{8,9},{9,10},{10,11},{12,13},{... | collective-permute-start | bytes 737288 | tf_op jit(solution)/shard_map/ppermute | solution.py:474
  12.1 38.6 %collective-permute-start.3 = (bf16[10,2,48,128]{3,2,1,0:T(8,128)(2,1)}, bf16[10,2,48,128]{3,2,1,0:T(8,128)(2,1)S(1)}, u32[]{:S(2)}, u32[]{:S(2)}) collective-permute-start(bf16[10,2,48,128]{3,2,1,0:T(8,128)(2,1)} %get-tuple-element.15.mine_low), channel_id=1, source_target_pairs={{1,0},{2,1},{3,2},{5,4},{6,5},{7,6},{9,8},{10,9},{11,10},{13,12},{... | collective-permute-start | bytes 737288 | tf_op jit(solution)/shard_map/ppermute | solution.py:475
  13.4 37.2 %collective-permute-start = (bf16[10,2,32,128]{3,2,1,0:T(8,128)(2,1)}, bf16[10,2,32,128]{3,2,1,0:T(8,128)(2,1)S(1)}, u32[]{:S(2)}, u32[]{:S(2)}) collective-permute-start(bf16[10,2,32,128]{3,2,1,0:T(8,128)(2,1)} %get-tuple-element.12), channel_id=1, source_target_pairs={{0,32},{32,64},{64,96},{1,33},{33,65},{65,97},{2,34},{34,66},{66,9... | collective-permute-start | bytes 491528 | tf_op jit(solution)/shard_map/ppermute | solution.py:476
  19.1 31.5 %collective-permute-start.1 = (bf16[10,2,32,128]{3,2,1,0:T(8,128)(2,1)}, bf16[10,2,32,128]{3,2,1,0:T(8,128)(2,1)S(1)}, u32[]{:S(2)}, u32[]{:S(2)}) collective-permute-start(bf16[10,2,32,128]{3,2,1,0:T(8,128)(2,1)} %get-tuple-element.13), channel_id=1, source_target_pairs={{32,0},{64,32},{96,64},{33,1},{65,33},{97,65},{34,2},{66,34},{98,6... | collective-permute-start | bytes 491528 | tf_op jit(solution)/shard_map/ppermute | solution.py:477
  21.0 8.3 %collective-permute-start.4 = (bf16[10,8,128]{2,1,0:T(8,128)(2,1)}, bf16[10,8,128]{2,1,0:T(8,128)(2,1)S(1)}, u32[]{:S(2)}, u32[]{:S(2)}) collective-permute-start(bf16[10,8,128]{2,1,0:T(8,128)(2,1)} %get-tuple-element.16), channel_id=1, source_target_pairs={{0,33},{1,34},{2,35},{32,65},{33,66},{34,67},{64,97},{65,98},{66,9... | collective-permute-start | bytes 61448 | tf_op jit(solution)/shard_map/ppermute | solution.py:486
  29.4 69.0 %copy-start.18 = (bf16[10,8,128]{2,1,0:T(8,128)(2,1)}, bf16[10,8,128]{2,1,0:T(8,128)(2,1)S(1)}, u32[]{:S(2)}) copy-start(bf16[10,8,128]{2,1,0:T(8,128)(2,1)S(1)} %collective-permute-done.4.c_ll) | copy-start | bytes 61444
  29.4 5.3 %collective-permute-start.5 = (bf16[10,8,128]{2,1,0:T(8,128)(2,1)}, bf16[10,8,128]{2,1,0:T(8,128)(2,1)S(1)}, u32[]{:S(2)}, u32[]{:S(2)}) collective-permute-start(bf16[10,8,128]{2,1,0:T(8,128)(2,1)} %get-tuple-element.17), channel_id=1, source_target_pairs={{1,32},{2,33},{3,34},{33,64},{34,65},{35,66},{65,96},{66,97},{67,9... | collective-permute-start | bytes 61448 | tf_op jit(solution)/shard_map/ppermute | solution.py:486
  34.7 63.7 %copy-start.20 = (bf16[10,8,128]{2,1,0:T(8,128)(2,1)}, bf16[10,8,128]{2,1,0:T(8,128)(2,1)S(1)}, u32[]{:S(2)}) copy-start(bf16[10,8,128]{2,1,0:T(8,128)(2,1)S(1)} %collective-permute-done.5.c_lr) | copy-start | bytes 61444
  34.7 3.0 %collective-permute-start.6 = (bf16[10,8,128]{2,1,0:T(8,128)(2,1)}, bf16[10,8,128]{2,1,0:T(8,128)(2,1)S(1)}, u32[]{:S(2)}, u32[]{:S(2)}) collective-permute-start(bf16[10,8,128]{2,1,0:T(8,128)(2,1)} %get-tuple-element.18), channel_id=1, source_target_pairs={{32,1},{33,2},{34,3},{64,33},{65,34},{66,35},{96,65},{97,66},{98,6... | collective-permute-start | bytes 61448 | tf_op jit(solution)/shard_map/ppermute | solution.py:486
  37.7 60.7 %copy-start.22 = (bf16[10,8,128]{2,1,0:T(8,128)(2,1)}, bf16[10,8,128]{2,1,0:T(8,128)(2,1)S(1)}, u32[]{:S(2)}) copy-start(bf16[10,8,128]{2,1,0:T(8,128)(2,1)S(1)} %collective-permute-done.6.c_rl) | copy-start | bytes 61444
  37.7 13.0 %collective-permute-start.7 = (bf16[10,8,128]{2,1,0:T(8,128)(2,1)}, bf16[10,8,128]{2,1,0:T(8,128)(2,1)S(1)}, u32[]{:S(2)}, u32[]{:S(2)}) collective-permute-start(bf16[10,8,128]{2,1,0:T(8,128)(2,1)} %get-tuple-element.19), channel_id=1, source_target_pairs={{33,0},{34,1},{35,2},{65,32},{66,33},{67,34},{97,64},{98,65},{99,6... | collective-permute-start | bytes 61448 | tf_op jit(solution)/shard_map/ppermute | solution.py:486
  50.6 47.7 %copy-start.24 = (bf16[10,8,128]{2,1,0:T(8,128)(2,1)}, bf16[10,8,128]{2,1,0:T(8,128)(2,1)S(1)}, u32[]{:S(2)}) copy-start(bf16[10,8,128]{2,1,0:T(8,128)(2,1)S(1)} %collective-permute-done.7.c_rr) | copy-start | bytes 61444
  50.7 47.7 %copy-start.14 = (bf16[10,2,32,128]{3,2,1,0:T(8,128)(2,1)}, bf16[10,2,32,128]{3,2,1,0:T(8,128)(2,1)S(1)}, u32[]{:S(2)}) copy-start(bf16[10,2,32,128]{3,2,1,0:T(8,128)(2,1)S(1)} %collective-permute-done.1.x_high) | copy-start | bytes 491524
  50.7 47.7 %copy-start.9 = (bf16[10,2,48,128]{3,2,1,0:T(8,128)(2,1)}, bf16[10,2,48,128]{3,2,1,0:T(8,128)(2,1)S(1)}, u32[]{:S(2)}) copy-start(bf16[10,2,48,128]{3,2,1,0:T(8,128)(2,1)S(1)} %collective-permute-done.2.y_low) | copy-start | bytes 737284
  50.7 1.3 copy-start.1
  52.0 1.1 copy-start.3
  53.1 0.9 copy-start.5
  54.0 0.9 copy-start.7
  55.0 0.8 copy-start.16
  55.8 0.7 copy-start.26
  56.5 41.9 %copy-start.11 = (bf16[10,2,48,128]{3,2,1,0:T(8,128)(2,1)}, bf16[10,2,48,128]{3,2,1,0:T(8,128)(2,1)S(1)}, u32[]{:S(2)}) copy-start(bf16[10,2,48,128]{3,2,1,0:T(8,128)(2,1)S(1)} %collective-permute-done.3.y_high) | copy-start | bytes 737284
  56.5 69.3 %copy-start.6 = (bf16[10,2,48,128]{3,2,1,0:T(8,128)(2,1)S(1)}, bf16[10,2,48,128]{3,2,1,0:T(8,128)(2,1)}, u32[]{:S(2)}) copy-start(bf16[10,2,48,128]{3,2,1,0:T(8,128)(2,1)} %get-tuple-element.15.mine_low) | copy-start | bytes 737284
  125.8 1.1 copy-start.2
  126.9 1.1 copy-start.4
  128.1 0.9 copy-start.8
  129.0 0.9 copy-start.10
  129.9 0.9 copy-start.12
  130.9 0.9 copy-start.15
  131.8 0.8 copy-start.17
  132.6 0.7 copy-start.19
  133.4 0.7 copy-start.21
  134.1 0.7 copy-start.23
  134.8 0.7 copy-start.25
  155.6 0.9 copy-start.13
